TPU v7x, 512 devices: a whole 4x8x8 slice. The times are simulated.
512 devices in a mesh: grid: 32 (over y_lo, z, core), occ: 16 (over x, y_hi).
Axes of the slice: x: 4, y: 8 (y_hi: 4, y_lo: 2; y = y_hi * 2 + y_lo), z: 8, core: 2. Of those that a mesh axis runs over, the one named last changes fastest.
Arguments:
- orbital_values: bfloat16 [8192, 16000], P('grid', 'occ'), may hold values from -6 to 6
- occupied: bfloat16 [16000, 512], P('occ', 'grid'), may hold values from -0.046875 to 0.046875
- trial: bfloat16 [16000, 512], P('occ', 'grid'), may hold values from -0.046875 to 0.046875
- point_weights: float32 [8192], P('grid'), may hold values from 0.1 to 1
- batch_sizes: int32 [256], P('grid'), may hold values from 1 to 32, 4096 in all
- significant: int32 [256, 128], P('grid', 'occ'), may hold values 0 or 1
Outputs:
- exchange: float32 [16000, 512], P('occ', 'grid')
Inputs may be any that keep to these rules, and one draw needn't show every extreme that they name: `batch_sizes`: batch sizes sum to 4096 and the largest is exactly 32.
All inputs are finite; a program needn't handle non-finite values. No bound on the sum of `batch_sizes` or of `significant` on one device may be relied on, other than what follows from the above.
Results may differ from a plain program's by a relative error of at most 0.0027.
Values may be sent and summed in bfloat16 or wider, within the bound.
A program may use at most 64 MiB of HBM per device.

v0:
```python
import math
import jax
import jax.numpy as jnp
from jax import lax
from jax.sharding import PartitionSpec as P


def screen(values, sizes, significant):
    rows, cols = values.shape
    batches = sizes.shape[0]
    blocks = significant.shape[1]
    blocked = (
        values.reshape(batches, rows // batches, blocks, cols // blocks)
        * significant.astype(values.dtype)[:, None, :, None]
    )
    position = lax.broadcasted_iota(jnp.int32, (batches, rows // batches), 1)
    live = (position < sizes[:, None]).astype(jnp.float32).reshape(rows)
    return (blocked.reshape(rows, cols), live)


def per_device(orbital_values, occupied, trial, point_weights, batch_sizes, significant):
    screened, live = screen(orbital_values, batch_sizes, significant)
    rows = screened.shape[0]
    grid_count = lax.axis_size("grid")
    columns = occupied.shape[1]
    total = columns * grid_count
    joined = jnp.concatenate((occupied, trial), axis=1)
    panels_all = lax.all_gather(joined, "grid", axis=1, tiled=True)
    terms = jnp.dot(screened, panels_all, preferred_element_type=jnp.float32)
    stacked = (
        terms.reshape(rows, grid_count, 2, columns).transpose(0, 2, 1, 3).reshape(rows, 2, total)
    )
    weight = point_weights * live
    occ_scale = 1.0 / math.sqrt(total)
    shares = lax.psum_scatter(stacked, "occ", scatter_dimension=2, tiled=True)
    orbitals = shares[:, 0]
    response = shares[:, 1]
    density = lax.psum(jnp.sum(orbitals * response, axis=1), "occ") * occ_scale
    kernel = (weight[:, None] * (density[:, None] * orbitals + response)).astype(jnp.bfloat16)
    kernel_all = lax.all_gather(kernel, "occ", axis=1, tiled=True)
    partial_value = lax.dot_general(
        screened, kernel_all, (((0,), (0,)), ((), ())), preferred_element_type=jnp.float32
    )
    npoints = rows * grid_count
    return lax.psum_scatter(partial_value, "grid", scatter_dimension=1, tiled=True) / math.sqrt(
        npoints
    )


def solution(mesh):
    placed = (
        P("grid", "occ"),
        P("occ", "grid"),
        P("occ", "grid"),
        P("grid"),
        P("grid"),
        P("grid", "occ"),
    )
    return jax.shard_map(
        per_device, mesh=mesh, in_specs=placed, out_specs=P("occ", "grid"), check_vma=False
    )
```

profile of v0, /device:TPU:2, one launch (start us, length us, event | category | flops | bytes accessed | tf_op | source)
XLA Modules:
  0.0 392.5 jit_solution(2788873274233231226)
XLA Ops:
  6.5 1.5 pad_maximum_fusion
  8.0 0.0 all-gather.2.cloned.1.call-update
  8.0 0.0 reduce-scatter.3.cloned.1.call-start
  8.1 0.7 convert_element_type.8
  8.8 0.1 mul.39
  8.9 0.4 mul.40
  9.3 0.2 copy.8
  9.6 0.2 mul.41
  9.8 71.9 %all-gather.2.cloned.1.call-done = bf16[1000,1024]{0,1:T(8,128)(2,1)} async-done(((bf16[1000,32]{0,1:T(8,128)(2,1)}), bf16[1000,1024]{0,1:T(8,128)(2,1)}) %all-gather.2.cloned.1.call-update) | async-done | bytes 2048016 | tf_op jit(solution)/shard_map/all_gather | solution.py:28
  81.7 3.1 fusion.2
  84.8 1.6 copy.11
  86.4 0.0 reduce-scatter.3.cloned.1.call-update
  86.4 0.0 reduce-scatter.5.cloned.1.call-start
  86.5 0.1 iota_compare_fusion
  86.6 0.1 lt.14
  86.7 91.1 %reduce-scatter.3.cloned.1.call-done = f32[256,2,32]{0,2,1:T(8,128)} async-done(((f32[256,2,512]{0,2,1:T(8,128)}), f32[256,2,32]{0,2,1:T(8,128)}) %reduce-scatter.3.cloned.1.call-update) | async-done | bytes 65552 | tf_op jit(solution)/shard_map/reduce_scatter | solution.py:35
  177.7 0.8 multiply_reduce_fusion
  178.5 38.1 %psum.7 = f32[256]{0:T(256)S(1)} all-reduce(f32[256]{0:T(256)S(1)} %multiply_reduce_fusion), channel_id=1, replica_groups=mesh['grid'=32,'occ'=16] {'occ'}, use_global_device_ids=true, to_apply=%region_2.0 | all-reduce | flops 256 | bytes 2048 | tf_op jit(solution)/shard_map/psum | solution.py:38
  216.6 0.8 multiply_convert_fusion
  217.4 39.4 %all_gather.7 = bf16[256,512]{0,1:T(8,128)(2,1)S(1)} all-gather(bf16[256,32]{0,1:T(8,128)(2,1)S(1)} %multiply_convert_fusion), channel_id=1, replica_groups=mesh['grid'=32,'occ'=16] {'occ'}, dimensions={1}, use_global_device_ids=true | all-gather | bytes 278528 | tf_op jit(solution)/shard_map/all_gather | solution.py:40
  256.7 1.8 fusion.6
  258.5 0.0 reduce-scatter.5.cloned.1.call-update
  258.6 125.9 %reduce-scatter.5.cloned.1.call-done = f32[1000,16]{0,1:T(8,128)} async-done(((f32[1000,512]{0,1:T(8,128)}), f32[1000,16]{0,1:T(8,128)}) %reduce-scatter.5.cloned.1.call-update) | async-done | bytes 64016 | tf_op jit(solution)/shard_map/reduce_scatter | solution.py:45
  384.5 1.5 broadcast_multiply_fusion
  (9 shorter events, 0.0 us)
Async XLA Ops:
  6.5 2.8 copy-start
  6.5 75.2 %all-gather.2.cloned.1.call-start = ((), (), s32[]{:S(2)}) async-start(), calls=%async_computation.2 | async-start | bytes 2162688 | tf_op jit(solution)/shard_map/all_gather | solution.py:28
  8.0 169.7 %reduce-scatter.3.cloned.1.call-start = ((), (), s32[]{:S(2)}) async-start(), calls=%async_computation.3 | async-start | bytes 1114112 | tf_op jit(solution)/shard_map/reduce_scatter | solution.py:35
  84.8 1.7 copy-start.2
  84.8 1.9 copy-start.1
  86.4 298.0 %reduce-scatter.5.cloned.1.call-start = ((), (), s32[]{:S(2)}) async-start(), calls=%async_computation.4 | async-start | bytes 2162688 | tf_op jit(solution)/shard_map/reduce_scatter | solution.py:45
Sparse Core Ops, SparseCore 0:
  9.5 72.1 all-gather.1
  86.6 91.1 reduce-scatter.2
  258.7 125.7 reduce-scatter.4
where the time goes:
time: 393 us; the launch traced here: 392 us
  waiting for transfers between devices  289 us (74%)
  blocking collectives  77.4 us (20%)
  between operations  13.2 us (3%)
  other arithmetic  5.49 us (1%)
  matrix products  4.87 us (1%)
    reduce_scatter x1, waiting for transfers between devices, per_device(): lax.psum_scatter(partial_value, 'grid', scatter_dimension=1, tiled=True)  126 us
    reduce_scatter x1, waiting for transfers between devices, per_device(): shares = lax.psum_scatter(stacked, 'occ', scatter_dimension=2, tiled=True)  91.1 us
    all_gather x1, waiting for transfers between devices, per_device(): panels_all = lax.all_gather(joined, 'grid', axis=1, tiled=True)  71.9 us
    all_gather x1, blocking collectives, per_device(): kernel_all = lax.all_gather(kernel, 'occ', axis=1, tiled=True)  39.4 us
    psum x1, blocking collectives, per_device(): density = lax.psum(jnp.sum(orbitals * response, axis=1), 'occ') * occ_scale  38.1 us
  transfers between devices with their start and end apart: 3, of which 3 were waited for; matrix products, arithmetic and copies ran while one was open for 0% of the time, Pallas kernels for 0%

commit v1 on v0

--- a/solution.py
+++ b/solution.py
@@ -37,7 +37,16 @@
     response = shares[:, 1]
     density = lax.psum(jnp.sum(orbitals * response, axis=1), "occ") * occ_scale
     kernel = (weight[:, None] * (density[:, None] * orbitals + response)).astype(jnp.bfloat16)
-    kernel_all = lax.all_gather(kernel, "occ", axis=1, tiled=True)
+
+    def finish_the_views(x0, named_axis, on_dim):
+        shelf = []
+        for _ in range(lax.axis_size(named_axis)):
+            shelf.append(x0)
+        return jnp.concatenate(
+            lax.all_to_all(jnp.stack(shelf, axis=0), named_axis, 0, 0), axis=on_dim
+        )
+
+    kernel_all = finish_the_views(kernel, "occ", 1)
     partial_value = lax.dot_general(
         screened, kernel_all, (((0,), (0,)), ((), ())), preferred_element_type=jnp.float32
     )

time: 393 us -> 367 us (0.934)
  blocking collectives: 77.4 us -> 56 us
  waiting for transfers between devices: 289 us -> 284 us
    all_gather x1 -> x0, blocking collectives: 39.4 us -> none  [per_device(): kernel_all = lax.all_gather(kernel, 'occ', axis=1, tiled=True)]
    all_to_all x0 -> x1, blocking collectives: none -> 17.9 us  [finish_the_views(): lax.all_to_all(jnp.stack(shelf, axis=0), named_axis, 0, 0)]
    reduce_scatter x1, waiting for transfers between devices: 126 us -> 121 us  [per_device(): lax.psum_scatter(partial_value, 'grid', scatter_dimension=1, tiled=True)]
where the time goes in v1:
time: 367 us; the launch traced here: 366 us
  waiting for transfers between devices  284 us (77%)
  blocking collectives  56 us (15%)
  between operations  13.2 us (4%)
  other arithmetic  5.49 us (1%)
  matrix products  4.88 us (1%)
    reduce_scatter x1, waiting for transfers between devices, per_device(): lax.psum_scatter(partial_value, 'grid', scatter_dimension=1, tiled=True)  121 us
    reduce_scatter x1, waiting for transfers between devices, per_device(): shares = lax.psum_scatter(stacked, 'occ', scatter_dimension=2, tiled=True)  91.1 us
    all_gather x1, waiting for transfers between devices, per_device(): panels_all = lax.all_gather(joined, 'grid', axis=1, tiled=True)  71.9 us
    psum x1, blocking collectives, per_device(): density = lax.psum(jnp.sum(orbitals * response, axis=1), 'occ') * occ_scale  38.1 us
    all_to_all x1, blocking collectives, finish_the_views(): lax.all_to_all(jnp.stack(shelf, axis=0), named_axis, 0, 0)  17.9 us
  transfers between devices with their start and end apart: 3, of which 3 were waited for; matrix products, arithmetic and copies ran while one was open for 0% of the time, Pallas kernels for 0%

profile of v1, /device:TPU:2, one launch (start us, length us, event | category | flops | bytes accessed | tf_op | source)
XLA Modules:
  0.0 366.1 jit_solution(7564510030865918474)
XLA Ops:
  6.5 1.5 pad_maximum_fusion
  8.0 0.0 all-gather.2.cloned.1.call-update
  8.0 0.0 reduce-scatter.3.cloned.1.call-start
  8.1 0.7 convert_element_type.10
  8.8 0.1 mul.43
  8.9 0.4 mul.44
  9.3 0.2 copy.8
  9.6 0.2 mul.45
  9.8 71.9 %all-gather.2.cloned.1.call-done = bf16[1000,1024]{0,1:T(8,128)(2,1)} async-done(((bf16[1000,32]{0,1:T(8,128)(2,1)}), bf16[1000,1024]{0,1:T(8,128)(2,1)}) %all-gather.2.cloned.1.call-update) | async-done | bytes 2048016 | tf_op jit(solution)/shard_map/all_gather | solution.py:28
  81.7 3.1 fusion.2
  84.8 1.6 copy.11
  86.4 0.0 reduce-scatter.3.cloned.1.call-update
  86.4 0.0 reduce-scatter.5.cloned.1.call-start
  86.5 0.1 iota_compare_fusion
  86.6 0.1 lt.14
  86.7 91.1 %reduce-scatter.3.cloned.1.call-done = f32[256,2,32]{0,2,1:T(8,128)} async-done(((f32[256,2,512]{0,2,1:T(8,128)}), f32[256,2,32]{0,2,1:T(8,128)}) %reduce-scatter.3.cloned.1.call-update) | async-done | bytes 65552 | tf_op jit(solution)/shard_map/reduce_scatter | solution.py:35
  177.7 0.8 multiply_reduce_fusion
  178.5 38.1 %psum.7 = f32[256]{0:T(256)S(1)} all-reduce(f32[256]{0:T(256)S(1)} %multiply_reduce_fusion), channel_id=1, replica_groups=mesh['grid'=32,'occ'=16] {'occ'}, use_global_device_ids=true, to_apply=%region_2.0 | all-reduce | flops 256 | bytes 2048 | tf_op jit(solution)/shard_map/psum | solution.py:38
  216.6 0.8 multiply_convert_fusion
  217.4 17.9 %all_to_all.5 = bf16[16,256,32]{1,2,0:T(8,128)(2,1)S(1)} all-to-all(bf16[16,256,32]{1,2,0:T(8,128)(2,1)S(1)} %stack.2), channel_id=1, replica_groups=mesh['grid'=32,'occ'=16] {'occ'}, dimensions={0} | all-to-all | bytes 524288 | tf_op jit(solution)/shard_map/all_to_all | solution.py:46
  235.3 1.8 fusion.6
  237.1 0.0 reduce-scatter.5.cloned.1.call-update
  237.2 120.9 %reduce-scatter.5.cloned.1.call-done = f32[1000,16]{0,1:T(8,128)} async-done(((f32[1000,512]{0,1:T(8,128)}), f32[1000,16]{0,1:T(8,128)}) %reduce-scatter.5.cloned.1.call-update) | async-done | bytes 64016 | tf_op jit(solution)/shard_map/reduce_scatter | solution.py:54
  358.1 1.5 broadcast_multiply_fusion
  (10 shorter events, 0.0 us)
Async XLA Ops:
  6.5 2.8 copy-start
  6.5 75.2 %all-gather.2.cloned.1.call-start = ((), (), s32[]{:S(2)}) async-start(), calls=%async_computation.3 | async-start | bytes 2162688 | tf_op jit(solution)/shard_map/all_gather | solution.py:28
  8.0 169.7 %reduce-scatter.3.cloned.1.call-start = ((), (), s32[]{:S(2)}) async-start(), calls=%async_computation.4 | async-start | bytes 1114112 | tf_op jit(solution)/shard_map/reduce_scatter | solution.py:35
  84.8 1.7 copy-start.2
  84.8 1.9 copy-start.1
  86.4 271.7 %reduce-scatter.5.cloned.1.call-start = ((), (), s32[]{:S(2)}) async-start(), calls=%async_computation.5 | async-start | bytes 2162688 | tf_op jit(solution)/shard_map/reduce_scatter | solution.py:54
Sparse Core Ops, SparseCore 0:
  9.5 72.1 all-gather.1
  86.6 91.1 reduce-scatter.2
  237.3 120.7 reduce-scatter.4
